TPU v7x, 256 devices: a whole 4x4x8 slice. The times are simulated.
256 devices in a mesh: dom: 64 (over z, y, core), grp: 4 (over x).
Axes of the slice: x: 4, y: 4, z: 8, core: 2. Of those that a mesh axis runs over, the one named last changes fastest.
Arguments:
- element_faces: int32 [4, 8192], P(None, 'dom'), may hold values from 0 to 8191, as said below
- interior_load: bfloat16 [80, 8192], P(None, 'dom'), may hold values from -6 to 6
- inverses: bfloat16 [80, 80, 8192], P('grp', None, 'dom'), may hold values from -0.625 to 0.625
- lift_operator: float32 [80, 240], P('grp'), may hold values from -0.625 to 0.625
- face_area: float32 [4, 8192], P(None, 'dom'), may hold values from 0.3 to 27
- columns: int32 [7, 8192], P(None, 'dom'), may hold values from -1 to 8191, as said below
- blocks: float32 [7, 60, 60, 8192], P(None, 'grp', None, 'dom'), may hold values from -0.00119 to 0.00119
- diagonal: float32 [60, 8192], P('grp', 'dom'), may hold values from 1.02 to 1.3
Outputs:
- solution: float32 [60, 8192], P('grp', 'dom')
- residual: float32 [60, 8192], P('grp', 'dom')
Inputs may be any that keep to these rules, and one draw needn't show every extreme that they name: `element_faces`: every face block of an element is owned by the element's own index of dom or the one before or after it; an index owns the face blocks i * 128 to (i + 1) * 128 - 1. `columns`: slot 0 of a face block row holds the block itself. Every other nonnegative entry is a face block owned by the row's own index of dom or the one before or after it, and within one slot no number appears twice.
All inputs are finite; a program needn't handle non-finite values.
Results may differ from a plain program's by a relative error of at most 0.0003.
Values sent between devices are 32-bit elements; how exact they have to be, the bound alone decides.
A program may use at most 64 MiB of HBM per device.

v0:
```python
import jax
import jax.numpy as jnp
from jax import lax
from jax.sharding import Mesh
from jax.sharding import PartitionSpec as P

ITERS = 8
DOM = ("dom_0", "dom_1", "dom_2")
DOM_GRP = ("dom_0", "dom_1", "dom_2", "grp")


def in_order(blocks, dim):
    blocks = jnp.moveaxis(blocks, 0, dim)
    dims = blocks.shape
    return blocks.reshape(*dims[:dim], dims[dim] * dims[dim + 1], *dims[dim + 2 :])


def copy_for_each(value, axis):
    copies = jnp.broadcast_to(value, (lax.axis_size(axis), *value.shape))
    return lax.all_to_all(copies, axis, split_axis=0, concat_axis=0, tiled=True)


def gather_directly(value, axis, dim):
    return in_order(copy_for_each(value, axis), dim)


def padded(cells, sides, width):
    for axis, dim in sides:
        count = lax.axis_size(axis)
        ends = count - 1
        head = lax.slice_in_dim(cells, 0, width, axis=dim)
        tail = lax.slice_in_dim(cells, cells.shape[dim] - width, cells.shape[dim], axis=dim)
        cells = jnp.concatenate(
            [
                lax.ppermute(tail, axis, [(i, (i + 1) % count) for i in range(ends)]),
                cells,
                lax.ppermute(head, axis, [((i + 1) % count, i) for i in range(ends)]),
            ],
            axis=dim,
        )
    return cells


def shifted(block, axis, distance):
    devices = range(lax.axis_size(axis))
    route = [(i - distance, i) for i in devices if i - distance in devices]
    return lax.ppermute(block, axis, route)


def cut_along(value, dim, count):
    before, after = (value.shape[:dim], value.shape[dim + 1 :])
    return jnp.moveaxis(value.reshape(*before, count, -1, *after), dim, 0)


def summed_on_arrival(value, axis, dim):
    count = lax.axis_size(axis)
    blocks = lax.all_to_all(cut_along(value, dim, count), axis, 0, 0, tiled=True)
    return jnp.sum(blocks, axis=0)


def by_axis(value, axes):
    for axis in axes:
        value = lax.psum(value, axis)
    return value


def spread(field_rows):
    faces_here = field_rows.shape[1]
    whole = gather_directly(field_rows, "grp", 0)
    return padded(whole, ((DOM, 1),), faces_here)


def deliver(slab):
    faces_here = slab.shape[1] // 3
    from_upper = shifted(slab[:, :faces_here], DOM, -1)
    from_lower = shifted(slab[:, 2 * faces_here :], DOM, 1)
    summed = slab[:, faces_here : 2 * faces_here] + from_upper + from_lower
    return summed_on_arrival(summed, "grp", 0)


def to_slab(entries, targets, faces_here):
    return jax.ops.segment_sum(entries, targets.reshape(-1), num_segments=3 * faces_here).T


def operate(field_rows, blocks, local_index, usable, diagonal):
    slab = spread(field_rows)
    picked = jnp.where(usable[None, :, :], slab[:, local_index], jnp.zeros((), jnp.float32))
    forward = jnp.einsum("sijf,jsf->if", blocks, picked, precision=lax.Precision.HIGHEST)
    transposed = jnp.einsum("sijf,if->sjf", blocks, field_rows, precision=lax.Precision.HIGHEST)
    transposed = jnp.where(usable[:, None, :], transposed, jnp.zeros((), jnp.float32))
    slot_count, height, faces_here = transposed.shape
    entries = jnp.transpose(transposed, (0, 2, 1)).reshape(slot_count * faces_here, height)
    return diagonal * field_rows + forward + deliver(to_slab(entries, local_index, faces_here))


def two_products(residual, image):
    return (
        by_axis(jnp.sum(residual * residual), DOM_GRP),
        by_axis(jnp.sum(residual * image), DOM_GRP),
    )


def on_device(
    element_faces, interior_load, inverses, lift_operator, face_area, columns, blocks, diagonal
):
    domain = lax.axis_index(DOM)
    faces_here = diagonal.shape[1]
    full_width = lift_operator.shape[1] // 4
    elements_here = interior_load.shape[1]
    u_rows = jnp.einsum("ije,je->ie", inverses, interior_load, preferred_element_type=jnp.float32)
    lifted = lax.dot_general(
        lift_operator, u_rows, (((0,), (0,)), ((), ())), precision=lax.Precision.HIGHEST
    )
    contrib = -(lifted.reshape(4, full_width, elements_here) * face_area[:, None, :])
    entries = jnp.transpose(contrib, (0, 2, 1)).reshape(4 * elements_here, full_width)
    slot_faces = element_faces - (domain - 1) * faces_here
    right_side = deliver(to_slab(entries, slot_faces, faces_here))
    usable = columns >= 0
    local_index = jnp.where(usable, columns - (domain - 1) * faces_here, faces_here)
    solution = jnp.zeros_like(right_side)
    residual = right_side
    image = operate(residual, blocks, local_index, usable, diagonal)
    norm_now, product_sum = two_products(residual, image)
    alpha = norm_now / product_sum
    direction, along = (residual, image)
    for iteration in range(ITERS):
        solution = solution + alpha * direction
        residual = residual - alpha * along
        if iteration + 1 < ITERS:
            image = operate(residual, blocks, local_index, usable, diagonal)
            norm_next, product_sum = two_products(residual, image)
            ratio = norm_next / norm_now
            alpha = norm_next / (product_sum - ratio * norm_next / alpha)
            direction = residual + ratio * direction
            along = image + ratio * along
            norm_now = norm_next
    return (solution, residual)


def solution(mesh):
    torus = Mesh(
        mesh.devices.reshape(8, 4, 2, mesh.shape["grp"]), ("dom_0", "dom_1", "dom_2", "grp")
    )
    placed = (
        P(None, DOM),
        P(None, DOM),
        P("grp", None, DOM),
        P("grp", None),
        P(None, DOM),
        P(None, DOM),
        P(None, "grp", None, DOM),
        P("grp", DOM),
    )
    return jax.shard_map(
        on_device,
        mesh=torus,
        in_specs=placed,
        out_specs=(P("grp", DOM), P("grp", DOM)),
        check_vma=False,
    )
```

profile of v0, /device:TPU:8, one launch (start us, length us, event | category | flops | bytes accessed | tf_op | source)
XLA Modules:
  0.0 880.3 jit_solution(18303853080815893465)
XLA Ops:
  20.0 4.8 all-to-all-done
  28.6 5.4 all-to-all-done.1
  53.7 7.1 scatter_custom_fusion.1
  77.8 4.0 all-to-all-done.2
  82.5 25.4 %all-reduce.7 = (f32[]{:T(128)}, f32[]{:T(128)}) all-reduce(f32[]{:T(128)} %get-tuple-element.17, f32[]{:T(128)} %get-tuple-element.16), channel_id=1, replica_groups=mesh['dom_0'=8,'dom_1'=4,'dom_2'=2,'grp'=4] {'dom_0'}, use_global_device_ids=true, to_apply=%region_3.4 | all-reduce | flops 2 | bytes 16 | tf_op jit(solution)/shard_map/psum | solution.py:63
  107.9 13.2 %all-reduce.23 = (f32[]{:T(128)}, f32[]{:T(128)}) all-reduce(f32[]{:T(128)} %get-tuple-element.32, f32[]{:T(128)} %get-tuple-element.33), channel_id=1, replica_groups=mesh['dom_0'=8,'dom_1'=4,'dom_2'=2,'grp'=4] {'dom_1'}, use_global_device_ids=true, to_apply=%region_4.5 | all-reduce | flops 2 | bytes 16 | tf_op jit(solution)/shard_map/psum | solution.py:63
  124.2 9.5 %all-reduce.15 = (f32[]{:T(128)}, f32[]{:T(128)}) all-reduce(f32[]{:T(128)} %get-tuple-element.80, f32[]{:T(128)} %get-tuple-element.81), channel_id=1, replica_groups=mesh['dom_0'=8,'dom_1'=4,'dom_2'=2,'grp'=4] {'grp'}, use_global_device_ids=true, to_apply=%region_6.7 | all-reduce | flops 2 | bytes 16 | tf_op jit(solution)/shard_map/psum | solution.py:63
  135.0 8.5 all_to_all.85
  163.1 7.1 scatter_custom_fusion.2
  186.2 4.1 all-to-all-done.4
  190.9 17.9 %all-reduce.6 = (f32[]{:T(128)}, f32[]{:T(128)}) all-reduce(f32[]{:T(128)} %get-tuple-element.15, f32[]{:T(128)} %get-tuple-element.14), channel_id=1, replica_groups=mesh['dom_0'=8,'dom_1'=4,'dom_2'=2,'grp'=4] {'dom_0'}, use_global_device_ids=true, to_apply=%region_15.16 | all-reduce | flops 2 | bytes 16 | tf_op jit(solution)/shard_map/psum | solution.py:63
  208.8 12.1 %all-reduce.22 = (f32[]{:T(128)}, f32[]{:T(128)}) all-reduce(f32[]{:T(128)} %get-tuple-element.30, f32[]{:T(128)} %get-tuple-element.31), channel_id=1, replica_groups=mesh['dom_0'=8,'dom_1'=4,'dom_2'=2,'grp'=4] {'dom_1'}, use_global_device_ids=true, to_apply=%region_16.17 | all-reduce | flops 2 | bytes 16 | tf_op jit(solution)/shard_map/psum | solution.py:63
  224.1 9.6 %all-reduce.14 = (f32[]{:T(128)}, f32[]{:T(128)}) all-reduce(f32[]{:T(128)} %get-tuple-element.78, f32[]{:T(128)} %get-tuple-element.79), channel_id=1, replica_groups=mesh['dom_0'=8,'dom_1'=4,'dom_2'=2,'grp'=4] {'grp'}, use_global_device_ids=true, to_apply=%region_18.19 | all-reduce | flops 2 | bytes 16 | tf_op jit(solution)/shard_map/psum | solution.py:63
  238.1 8.5 all_to_all.86
  266.2 7.1 scatter_custom_fusion.3
  289.3 4.1 all-to-all-done.6
  295.3 17.8 %all-reduce.5 = (f32[]{:T(128)}, f32[]{:T(128)}) all-reduce(f32[]{:T(128)} %get-tuple-element.13, f32[]{:T(128)} %get-tuple-element.12), channel_id=1, replica_groups=mesh['dom_0'=8,'dom_1'=4,'dom_2'=2,'grp'=4] {'dom_0'}, use_global_device_ids=true, to_apply=%region_27.28 | all-reduce | flops 2 | bytes 16 | tf_op jit(solution)/shard_map/psum | solution.py:63
  313.1 12.1 %all-reduce.21 = (f32[]{:T(128)}, f32[]{:T(128)}) all-reduce(f32[]{:T(128)} %get-tuple-element.28, f32[]{:T(128)} %get-tuple-element.29), channel_id=1, replica_groups=mesh['dom_0'=8,'dom_1'=4,'dom_2'=2,'grp'=4] {'dom_1'}, use_global_device_ids=true, to_apply=%region_28.29 | all-reduce | flops 2 | bytes 16 | tf_op jit(solution)/shard_map/psum | solution.py:63
  328.4 9.5 %all-reduce.13 = (f32[]{:T(128)}, f32[]{:T(128)}) all-reduce(f32[]{:T(128)} %get-tuple-element.76, f32[]{:T(128)} %get-tuple-element.77), channel_id=1, replica_groups=mesh['dom_0'=8,'dom_1'=4,'dom_2'=2,'grp'=4] {'grp'}, use_global_device_ids=true, to_apply=%region_30.31 | all-reduce | flops 2 | bytes 16 | tf_op jit(solution)/shard_map/psum | solution.py:63
  342.4 8.5 all_to_all.87
  371.8 7.1 scatter_custom_fusion.4
  396.8 4.2 all-to-all-done.8
  402.4 17.8 %all-reduce.4 = (f32[]{:T(128)}, f32[]{:T(128)}) all-reduce(f32[]{:T(128)} %get-tuple-element.11, f32[]{:T(128)} %get-tuple-element.10), channel_id=1, replica_groups=mesh['dom_0'=8,'dom_1'=4,'dom_2'=2,'grp'=4] {'dom_0'}, use_global_device_ids=true, to_apply=%region_39.40 | all-reduce | flops 2 | bytes 16 | tf_op jit(solution)/shard_map/psum | solution.py:63
  420.2 12.1 %all-reduce.20 = (f32[]{:T(128)}, f32[]{:T(128)}) all-reduce(f32[]{:T(128)} %get-tuple-element.26, f32[]{:T(128)} %get-tuple-element.27), channel_id=1, replica_groups=mesh['dom_0'=8,'dom_1'=4,'dom_2'=2,'grp'=4] {'dom_1'}, use_global_device_ids=true, to_apply=%region_40.41 | all-reduce | flops 2 | bytes 16 | tf_op jit(solution)/shard_map/psum | solution.py:63
  435.4 9.6 %all-reduce.12 = (f32[]{:T(128)}, f32[]{:T(128)}) all-reduce(f32[]{:T(128)} %get-tuple-element.74, f32[]{:T(128)} %get-tuple-element.75), channel_id=1, replica_groups=mesh['dom_0'=8,'dom_1'=4,'dom_2'=2,'grp'=4] {'grp'}, use_global_device_ids=true, to_apply=%region_42.43 | all-reduce | flops 2 | bytes 16 | tf_op jit(solution)/shard_map/psum | solution.py:63
  448.9 8.5 all_to_all.88
  478.2 7.1 scatter_custom_fusion.5
  503.3 4.2 all-to-all-done.10
  508.9 17.8 %all-reduce.3 = (f32[]{:T(128)}, f32[]{:T(128)}) all-reduce(f32[]{:T(128)} %get-tuple-element.9, f32[]{:T(128)} %get-tuple-element.8), channel_id=1, replica_groups=mesh['dom_0'=8,'dom_1'=4,'dom_2'=2,'grp'=4] {'dom_0'}, use_global_device_ids=true, to_apply=%region_51.52 | all-reduce | flops 2 | bytes 16 | tf_op jit(solution)/shard_map/psum | solution.py:63
  526.7 12.1 %all-reduce.19 = (f32[]{:T(128)}, f32[]{:T(128)}) all-reduce(f32[]{:T(128)} %get-tuple-element.24, f32[]{:T(128)} %get-tuple-element.25), channel_id=1, replica_groups=mesh['dom_0'=8,'dom_1'=4,'dom_2'=2,'grp'=4] {'dom_1'}, use_global_device_ids=true, to_apply=%region_52.53 | all-reduce | flops 2 | bytes 16 | tf_op jit(solution)/shard_map/psum | solution.py:63
  542.0 9.5 %all-reduce.11 = (f32[]{:T(128)}, f32[]{:T(128)}) all-reduce(f32[]{:T(128)} %get-tuple-element.72, f32[]{:T(128)} %get-tuple-element.73), channel_id=1, replica_groups=mesh['dom_0'=8,'dom_1'=4,'dom_2'=2,'grp'=4] {'grp'}, use_global_device_ids=true, to_apply=%region_54.55 | all-reduce | flops 2 | bytes 16 | tf_op jit(solution)/shard_map/psum | solution.py:63
  556.0 8.5 all_to_all.89
  585.4 7.1 scatter_custom_fusion.6
  610.4 4.2 all-to-all-done.12
  617.3 17.8 %all-reduce.2 = (f32[]{:T(128)}, f32[]{:T(128)}) all-reduce(f32[]{:T(128)} %get-tuple-element.7, f32[]{:T(128)} %get-tuple-element.6), channel_id=1, replica_groups=mesh['dom_0'=8,'dom_1'=4,'dom_2'=2,'grp'=4] {'dom_0'}, use_global_device_ids=true, to_apply=%region_63.64 | all-reduce | flops 2 | bytes 16 | tf_op jit(solution)/shard_map/psum | solution.py:63
  635.1 12.1 %all-reduce.18 = (f32[]{:T(128)}, f32[]{:T(128)}) all-reduce(f32[]{:T(128)} %get-tuple-element.22, f32[]{:T(128)} %get-tuple-element.23), channel_id=1, replica_groups=mesh['dom_0'=8,'dom_1'=4,'dom_2'=2,'grp'=4] {'dom_1'}, use_global_device_ids=true, to_apply=%region_64.65 | all-reduce | flops 2 | bytes 16 | tf_op jit(solution)/shard_map/psum | solution.py:63
  650.3 9.5 %all-reduce.10 = (f32[]{:T(128)}, f32[]{:T(128)}) all-reduce(f32[]{:T(128)} %get-tuple-element.70, f32[]{:T(128)} %get-tuple-element.71), channel_id=1, replica_groups=mesh['dom_0'=8,'dom_1'=4,'dom_2'=2,'grp'=4] {'grp'}, use_global_device_ids=true, to_apply=%region_66.67 | all-reduce | flops 2 | bytes 16 | tf_op jit(solution)/shard_map/psum | solution.py:63
  663.5 8.5 all_to_all.90
  692.9 7.1 scatter_custom_fusion.7
  718.0 4.2 all-to-all-done.14
  723.6 17.8 %all-reduce.1 = (f32[]{:T(128)}, f32[]{:T(128)}) all-reduce(f32[]{:T(128)} %get-tuple-element.5, f32[]{:T(128)} %get-tuple-element.4), channel_id=1, replica_groups=mesh['dom_0'=8,'dom_1'=4,'dom_2'=2,'grp'=4] {'dom_0'}, use_global_device_ids=true, to_apply=%region_75.76 | all-reduce | flops 2 | bytes 16 | tf_op jit(solution)/shard_map/psum | solution.py:63
  741.4 12.1 %all-reduce.17 = (f32[]{:T(128)}, f32[]{:T(128)}) all-reduce(f32[]{:T(128)} %get-tuple-element.20, f32[]{:T(128)} %get-tuple-element.21), channel_id=1, replica_groups=mesh['dom_0'=8,'dom_1'=4,'dom_2'=2,'grp'=4] {'dom_1'}, use_global_device_ids=true, to_apply=%region_76.77 | all-reduce | flops 2 | bytes 16 | tf_op jit(solution)/shard_map/psum | solution.py:63
  756.6 9.5 %all-reduce.9 = (f32[]{:T(128)}, f32[]{:T(128)}) all-reduce(f32[]{:T(128)} %get-tuple-element.68, f32[]{:T(128)} %get-tuple-element.69), channel_id=1, replica_groups=mesh['dom_0'=8,'dom_1'=4,'dom_2'=2,'grp'=4] {'grp'}, use_global_device_ids=true, to_apply=%region_78.79 | all-reduce | flops 2 | bytes 16 | tf_op jit(solution)/shard_map/psum | solution.py:63
  770.7 8.5 all_to_all.91
  800.1 7.1 scatter_custom_fusion.8
  831.4 17.8 %all-reduce = (f32[]{:T(128)}, f32[]{:T(128)}) all-reduce(f32[]{:T(128)} %get-tuple-element.3, f32[]{:T(128)} %get-tuple-element.2), channel_id=1, replica_groups=mesh['dom_0'=8,'dom_1'=4,'dom_2'=2,'grp'=4] {'dom_0'}, use_global_device_ids=true, to_apply=%region_87.88 | all-reduce | flops 2 | bytes 16 | tf_op jit(solution)/shard_map/psum | solution.py:63
  849.2 12.1 %all-reduce.16 = (f32[]{:T(128)}, f32[]{:T(128)}) all-reduce(f32[]{:T(128)} %get-tuple-element.18, f32[]{:T(128)} %get-tuple-element.19), channel_id=1, replica_groups=mesh['dom_0'=8,'dom_1'=4,'dom_2'=2,'grp'=4] {'dom_1'}, use_global_device_ids=true, to_apply=%region_88.89 | all-reduce | flops 2 | bytes 16 | tf_op jit(solution)/shard_map/psum | solution.py:63
  864.5 9.6 %all-reduce.8 = (f32[]{:T(128)}, f32[]{:T(128)}) all-reduce(f32[]{:T(128)} %get-tuple-element.66, f32[]{:T(128)} %get-tuple-element.67), channel_id=1, replica_groups=mesh['dom_0'=8,'dom_1'=4,'dom_2'=2,'grp'=4] {'grp'}, use_global_device_ids=true, to_apply=%region_90.91 | all-reduce | flops 2 | bytes 16 | tf_op jit(solution)/shard_map/psum | solution.py:63
  (282 shorter events, 370.8 us)
Async XLA Ops:
  6.8 5.0 collective-permute-start
  8.7 6.1 collective-permute-start.1
  11.8 151.2 %copy-start.16 = (s32[896]{0:T(1024)}, s32[896]{0:T(1024)S(1)}, u32[]{:S(2)}) copy-start(s32[896]{0:T(1024)S(1)} %get-tuple-element.109) | copy-start | bytes 10756
  15.6 9.2 %all-to-all-start = ((f32[4,15,128]{2,1,0:T(8,128)}), f32[4,15,128]{2,1,0:T(8,128)S(1)}, u32[]{:S(2)}, u32[]{:S(2)}) async-start(f32[4,15,128]{2,1,0:T(8,128)} %reshape.90), calls=%async_computation | async-start | bytes 65536 | tf_op jit(solution)/shard_map/all_to_all | solution.py:57
  25.4 8.7 all-to-all-start.1
  34.8 7.4 collective-permute-start.3
  36.7 5.8 collective-permute-start.2
  61.7 6.5 collective-permute-start.4
  64.5 5.6 collective-permute-start.5
  73.2 8.7 all-to-all-start.2
  145.0 5.6 collective-permute-start.7
  147.0 5.8 collective-permute-start.6
  171.0 6.5 collective-permute-start.8
  172.9 5.6 collective-permute-start.9
  181.5 8.7 all-to-all-start.4
  248.1 5.6 collective-permute-start.11
  250.1 5.8 collective-permute-start.10
  274.1 6.0 collective-permute-start.12
  276.0 5.6 collective-permute-start.13
  284.7 8.7 all-to-all-start.6
  342.4 106.5 %copy-start.15 = (f32[15,128]{1,0:T(8,128)}, f32[15,128]{1,0:T(8,128)S(1)}, u32[]{:S(2)}) copy-start(f32[15,128]{1,0:T(8,128)S(1)} %get-tuple-element.87) | copy-start | bytes 23044
  353.7 5.6 collective-permute-start.15
  355.7 5.8 collective-permute-start.14
  379.7 6.0 collective-permute-start.16
  381.6 5.6 collective-permute-start.17
  391.6 9.4 %all-to-all-start.8 = ((f32[4,15,128]{2,1,0:T(8,128)}), f32[4,15,128]{2,1,0:T(8,128)}, u32[]{:S(2)}, u32[]{:S(2)}) async-start(f32[4,15,128]{2,1,0:T(8,128)} %reshape.102), calls=%async_computation.8 | async-start | bytes 65536 | tf_op jit(solution)/shard_map/all_to_all | solution.py:57
  460.2 5.7 collective-permute-start.19
  462.2 5.8 collective-permute-start.18
  486.2 6.0 collective-permute-start.20
  488.1 5.6 collective-permute-start.21
  498.1 9.4 %all-to-all-start.10 = ((f32[4,15,128]{2,1,0:T(8,128)}), f32[4,15,128]{2,1,0:T(8,128)}, u32[]{:S(2)}, u32[]{:S(2)}) async-start(f32[4,15,128]{2,1,0:T(8,128)} %reshape.105), calls=%async_computation.10 | async-start | bytes 65536 | tf_op jit(solution)/shard_map/all_to_all | solution.py:57
  556.0 107.5 %copy-start.12 = (f32[15,128]{1,0:T(8,128)}, f32[15,128]{1,0:T(8,128)S(1)}, u32[]{:S(2)}) copy-start(f32[15,128]{1,0:T(8,128)S(1)} %get-tuple-element.84) | copy-start | bytes 23044
  567.3 5.6 collective-permute-start.23
  569.3 5.8 collective-permute-start.22
  593.3 6.0 collective-permute-start.24
  595.2 5.6 collective-permute-start.25
  605.2 9.4 %all-to-all-start.12 = ((f32[4,15,128]{2,1,0:T(8,128)}), f32[4,15,128]{2,1,0:T(8,128)}, u32[]{:S(2)}, u32[]{:S(2)}) async-start(f32[4,15,128]{2,1,0:T(8,128)} %reshape.108), calls=%async_computation.12 | async-start | bytes 65536 | tf_op jit(solution)/shard_map/all_to_all | solution.py:57
  617.3 71.7 %copy-start.10 = (f32[15,128]{1,0:T(8,128)}, f32[15,128]{1,0:T(8,128)S(1)}, u32[]{:S(2)}) copy-start(f32[15,128]{1,0:T(8,128)S(1)} %get-tuple-element.82) | copy-start | bytes 23044
  674.9 5.8 collective-permute-start.27
  676.9 5.8 collective-permute-start.26
  700.9 6.0 collective-permute-start.28
  702.8 5.6 collective-permute-start.29
  712.8 9.4 %all-to-all-start.14 = ((f32[4,15,128]{2,1,0:T(8,128)}), f32[4,15,128]{2,1,0:T(8,128)}, u32[]{:S(2)}, u32[]{:S(2)}) async-start(f32[4,15,128]{2,1,0:T(8,128)} %reshape.111), calls=%async_computation.14 | async-start | bytes 65536 | tf_op jit(solution)/shard_map/all_to_all | solution.py:57
  782.0 5.6 collective-permute-start.31
  784.0 5.8 collective-permute-start.30
  808.0 6.0 collective-permute-start.32
  809.9 5.6 collective-permute-start.33
  819.9 9.4 %all-to-all-start.16 = ((f32[4,15,128]{2,1,0:T(8,128)}), f32[4,15,128]{2,1,0:T(8,128)}, u32[]{:S(2)}, u32[]{:S(2)}) async-start(f32[4,15,128]{2,1,0:T(8,128)} %reshape.114), calls=%async_computation.16 | async-start | bytes 65536 | tf_op jit(solution)/shard_map/all_to_all | solution.py:57
  (13 other events, 287.1 us)
where the time goes:
time: 897 us; the launch traced here: 880 us
  blocking collectives  409 us (46%)
  other arithmetic  137 us (15%)
  local copies, waits for them, and re-layouts  119 us (13%)
  starting transfers between devices  112 us (12%)
  waiting for transfers between devices  73.5 us (8%)
  between operations  30.3 us (3%)
    psum x32, blocking collectives, by_axis(): value = lax.psum(value, axis)  349 us
    all_to_all x7, blocking collectives, copy_for_each(): return lax.all_to_all(copies, axis, split_axis=0, concat_axis=0, tiled=True)  59.4 us
    scatter-add x9, other arithmetic, to_slab(): jax.ops.segment_sum(entries, targets.reshape(-1), num_segments=3 * faces_...  58.8 us
    gather x16, local copies, waits for them, and re-layouts, operate(): slab[:, local_index]  44.8 us
    ppermute x18, starting transfers between devices, shifted(): return lax.ppermute(block, axis, route)  39.9 us
    all_to_all x9, waiting for transfers between devices, summed_on_arrival(): lax.all_to_all(cut_along(value, dim, count), axis, 0, 0, tiled=True)  37.1 us
    all_to_all x9, starting transfers between devices, summed_on_arrival(): lax.all_to_all(cut_along(value, dim, count), axis, 0, 0, tiled=True)  32.8 us
    unnamed x17, other arithmetic  27.6 us
  transfers between devices with their start and end apart: 44, of which 27 were waited for; matrix products, arithmetic and copies ran while one was open for 4% of the time, Pallas kernels for 0%

commit v1 on v0

--- a/solution.py
+++ b/solution.py
@@ -60,7 +60,7 @@
 
 def by_axis(value, axes):
     for axis in axes:
-        value = lax.psum(value, axis)
+        value = jnp.sum(lax.all_gather(value, axis), axis=0)
     return value
 
 

time: 897 us -> 1040 us (1.16)
  local copies, waits for them, and re-layouts: 119 us -> 238 us
  other arithmetic: 137 us -> 182 us
  blocking collectives: 409 us -> 391 us
    psum x32 -> x0, blocking collectives: 349 us -> none  [by_axis(): value = lax.psum(value, axis)]
    unnamed x0 -> x32, blocking collectives: none -> 332 us
    unnamed x42 -> x194, local copies, waits for them, and re-layouts: 13.3 us -> 132 us
    reduce_sum x0 -> x64, other arithmetic: none -> 44.8 us  [by_axis(): value = jnp.sum(lax.all_gather(value, axis), axis=0)]
where the time goes in v1:
time: 1040 us; the launch traced here: 1030 us
  blocking collectives  391 us (38%)
  local copies, waits for them, and re-layouts  238 us (23%)
  other arithmetic  182 us (18%)
  starting transfers between devices  112 us (11%)
  waiting for transfers between devices  73.8 us (7%)
  between operations  31.3 us (3%)
    unnamed x32, blocking collectives  332 us
    unnamed x194, local copies, waits for them, and re-layouts  132 us
    all_to_all x7, blocking collectives, copy_for_each(): return lax.all_to_all(copies, axis, split_axis=0, concat_axis=0, tiled=True)  59.4 us
    scatter-add x9, other arithmetic, to_slab(): jax.ops.segment_sum(entries, targets.reshape(-1), num_segments=3 * faces_...  59 us
    gather x16, local copies, waits for them, and re-layouts, operate(): slab[:, local_index]  44.8 us
    reduce_sum x64, other arithmetic, by_axis(): value = jnp.sum(lax.all_gather(value, axis), axis=0)  44.8 us
    ppermute x18, starting transfers between devices, shifted(): return lax.ppermute(block, axis, route)  39.4 us
    all_to_all x9, waiting for transfers between devices, summed_on_arrival(): lax.all_to_all(cut_along(value, dim, count), axis, 0, 0, tiled=True)  37.1 us
  transfers between devices with their start and end apart: 44, of which 27 were waited for; matrix products, arithmetic and copies ran while one was open for 4% of the time, Pallas kernels for 0%

profile of v1, /device:TPU:8, one launch (start us, length us, event | category | flops | bytes accessed | tf_op | source)
XLA Modules:
  0.0 1028.0 jit_solution(3661521938234476110)
XLA Ops:
  20.0 4.8 all-to-all-done
  28.7 5.4 all-to-all-done.1
  53.7 7.1 scatter_custom_fusion.1
  87.5 24.8 %all-reduce.71 = (f32[8]{0:T(128)S(1)}, f32[8]{0:T(128)S(1)}) all-reduce(f32[8]{0:T(128)S(1)} %dynamic-update-slice, f32[8]{0:T(128)S(1)} %dynamic-update-slice.4), channel_id=1, replica_groups=mesh['dom_0'=8,'dom_1'=4,'dom_2'=2,'grp'=4] {'dom_0'}, use_global_device_ids=true, to_apply=%add | all-reduce | flops 16 | bytes 128
  117.5 12.5 %all-reduce.87 = (f32[4]{0:T(128)S(1)}, f32[4]{0:T(128)S(1)}) all-reduce(f32[4]{0:T(128)S(1)} %dynamic-update-slice.1, f32[4]{0:T(128)S(1)} %dynamic-update-slice.5), channel_id=1, replica_groups=mesh['dom_0'=8,'dom_1'=4,'dom_2'=2,'grp'=4] {'dom_1'}, use_global_device_ids=true, to_apply=%add.1 | all-reduce | flops 8 | bytes 64
  141.0 8.9 all-reduce.79
  152.4 8.5 all_to_all.85
  180.5 7.1 scatter_custom_fusion.2
  203.6 4.1 all-to-all-done.4
  211.1 17.1 %all-reduce.70 = (f32[8]{0:T(128)S(1)}, f32[8]{0:T(128)S(1)}) all-reduce(f32[8]{0:T(128)S(1)} %dynamic-update-slice.8, f32[8]{0:T(128)S(1)} %dynamic-update-slice.12), channel_id=1, replica_groups=mesh['dom_0'=8,'dom_1'=4,'dom_2'=2,'grp'=4] {'dom_0'}, use_global_device_ids=true, to_apply=%add.8 | all-reduce | flops 16 | bytes 128
  232.3 11.4 %all-reduce.86 = (f32[4]{0:T(128)S(1)}, f32[4]{0:T(128)S(1)}) all-reduce(f32[4]{0:T(128)S(1)} %dynamic-update-slice.9, f32[4]{0:T(128)S(1)} %dynamic-update-slice.13), channel_id=1, replica_groups=mesh['dom_0'=8,'dom_1'=4,'dom_2'=2,'grp'=4] {'dom_1'}, use_global_device_ids=true, to_apply=%add.9 | all-reduce | flops 8 | bytes 64
  254.6 8.9 all-reduce.78
  269.3 8.5 all_to_all.86
  297.3 7.1 scatter_custom_fusion.3
  320.5 4.1 all-to-all-done.6
  329.3 17.1 %all-reduce.69 = (f32[8]{0:T(128)S(1)}, f32[8]{0:T(128)S(1)}) all-reduce(f32[8]{0:T(128)S(1)} %dynamic-update-slice.16, f32[8]{0:T(128)S(1)} %dynamic-update-slice.20), channel_id=1, replica_groups=mesh['dom_0'=8,'dom_1'=4,'dom_2'=2,'grp'=4] {'dom_0'}, use_global_device_ids=true, to_apply=%add.16 | all-reduce | flops 16 | bytes 128
  350.2 11.4 %all-reduce.85 = (f32[4]{0:T(128)S(1)}, f32[4]{0:T(128)S(1)}) all-reduce(f32[4]{0:T(128)S(1)} %dynamic-update-slice.17, f32[4]{0:T(128)S(1)} %dynamic-update-slice.21), channel_id=1, replica_groups=mesh['dom_0'=8,'dom_1'=4,'dom_2'=2,'grp'=4] {'dom_1'}, use_global_device_ids=true, to_apply=%add.17 | all-reduce | flops 8 | bytes 64
  372.2 8.9 all-reduce.77
  387.0 8.5 all_to_all.87
  416.4 7.1 scatter_custom_fusion.4
  441.5 4.2 all-to-all-done.8
  449.9 17.1 %all-reduce.68 = (f32[8]{0:T(128)S(1)}, f32[8]{0:T(128)S(1)}) all-reduce(f32[8]{0:T(128)S(1)} %dynamic-update-slice.24, f32[8]{0:T(128)S(1)} %dynamic-update-slice.28), channel_id=1, replica_groups=mesh['dom_0'=8,'dom_1'=4,'dom_2'=2,'grp'=4] {'dom_0'}, use_global_device_ids=true, to_apply=%add.24 | all-reduce | flops 16 | bytes 128
  470.9 11.4 %all-reduce.84 = (f32[4]{0:T(128)S(1)}, f32[4]{0:T(128)S(1)}) all-reduce(f32[4]{0:T(128)S(1)} %dynamic-update-slice.25, f32[4]{0:T(128)S(1)} %dynamic-update-slice.29), channel_id=1, replica_groups=mesh['dom_0'=8,'dom_1'=4,'dom_2'=2,'grp'=4] {'dom_1'}, use_global_device_ids=true, to_apply=%add.25 | all-reduce | flops 8 | bytes 64
  492.7 8.9 all-reduce.76
  506.7 8.5 all_to_all.88
  536.1 7.1 scatter_custom_fusion.5
  555.9 4.3 all-to-all-start.10
  561.6 4.1 all-to-all-done.10
  571.6 17.2 %all-reduce.67 = (f32[8]{0:T(128)S(1)}, f32[8]{0:T(128)S(1)}) all-reduce(f32[8]{0:T(128)} %dynamic-update-slice.32, f32[8]{0:T(128)} %copy-done.19), channel_id=1, replica_groups=mesh['dom_0'=8,'dom_1'=4,'dom_2'=2,'grp'=4] {'dom_0'}, use_global_device_ids=true, to_apply=%add.32 | all-reduce | flops 16 | bytes 128
  594.5 11.6 %all-reduce.83 = (f32[4]{0:T(128)S(1)}, f32[4]{0:T(128)S(1)}) all-reduce(f32[4]{0:T(128)} %dynamic-update-slice.33, f32[4]{0:T(128)} %copy-done.20), channel_id=1, replica_groups=mesh['dom_0'=8,'dom_1'=4,'dom_2'=2,'grp'=4] {'dom_1'}, use_global_device_ids=true, to_apply=%add.33 | all-reduce | flops 8 | bytes 64
  620.0 9.0 all-reduce.75
  635.0 8.5 all_to_all.89
  664.4 7.1 scatter_custom_fusion.6
  689.4 4.2 all-to-all-done.12
  700.8 17.2 %all-reduce.66 = (f32[8]{0:T(128)S(1)}, f32[8]{0:T(128)S(1)}) all-reduce(f32[8]{0:T(128)} %dynamic-update-slice.40, f32[8]{0:T(128)} %copy-done.23), channel_id=1, replica_groups=mesh['dom_0'=8,'dom_1'=4,'dom_2'=2,'grp'=4] {'dom_0'}, use_global_device_ids=true, to_apply=%add.40 | all-reduce | flops 16 | bytes 128
  723.5 11.6 %all-reduce.82 = (f32[4]{0:T(128)S(1)}, f32[4]{0:T(128)S(1)}) all-reduce(f32[4]{0:T(128)} %dynamic-update-slice.41, f32[4]{0:T(128)} %copy-done.24), channel_id=1, replica_groups=mesh['dom_0'=8,'dom_1'=4,'dom_2'=2,'grp'=4] {'dom_1'}, use_global_device_ids=true, to_apply=%add.41 | all-reduce | flops 8 | bytes 64
  748.7 9.0 all-reduce.74
  762.9 8.5 all_to_all.90
  792.3 7.2 scatter_custom_fusion.7
  817.5 4.2 all-to-all-done.14
  829.3 17.8 %all-reduce.65 = (f32[8]{0:T(128)}, f32[8]{0:T(128)}) all-reduce(f32[8]{0:T(128)} %dynamic-update-slice.48, f32[8]{0:T(128)} %dynamic-update-slice.52), channel_id=1, replica_groups=mesh['dom_0'=8,'dom_1'=4,'dom_2'=2,'grp'=4] {'dom_0'}, use_global_device_ids=true, to_apply=%add.48 | all-reduce | flops 16 | bytes 128
  855.7 12.1 %all-reduce.81 = (f32[4]{0:T(128)}, f32[4]{0:T(128)}) all-reduce(f32[4]{0:T(128)} %dynamic-update-slice.49, f32[4]{0:T(128)} %dynamic-update-slice.53), channel_id=1, replica_groups=mesh['dom_0'=8,'dom_1'=4,'dom_2'=2,'grp'=4] {'dom_1'}, use_global_device_ids=true, to_apply=%add.49 | all-reduce | flops 8 | bytes 64
  888.3 9.6 all-reduce.73
  905.3 8.5 all_to_all.91
  934.7 7.1 scatter_custom_fusion.8
  968.8 17.1 %all-reduce.64 = (f32[8]{0:T(128)S(1)}, f32[8]{0:T(128)S(1)}) all-reduce(f32[8]{0:T(128)S(1)} %dynamic-update-slice.56, f32[8]{0:T(128)S(1)} %dynamic-update-slice.60), channel_id=1, replica_groups=mesh['dom_0'=8,'dom_1'=4,'dom_2'=2,'grp'=4] {'dom_0'}, use_global_device_ids=true, to_apply=%add.56 | all-reduce | flops 16 | bytes 128
  989.7 11.4 %all-reduce.80 = (f32[4]{0:T(128)S(1)}, f32[4]{0:T(128)S(1)}) all-reduce(f32[4]{0:T(128)S(1)} %dynamic-update-slice.57, f32[4]{0:T(128)S(1)} %dynamic-update-slice.61), channel_id=1, replica_groups=mesh['dom_0'=8,'dom_1'=4,'dom_2'=2,'grp'=4] {'dom_1'}, use_global_device_ids=true, to_apply=%add.57 | all-reduce | flops 8 | bytes 64
  1011.5 8.9 all-reduce.72
  (498 shorter events, 530.4 us)
Async XLA Ops:
  6.8 5.0 collective-permute-start
  8.7 6.1 collective-permute-start.1
  11.8 168.7 %copy-start.16 = (s32[896]{0:T(1024)}, s32[896]{0:T(1024)S(1)}, u32[]{:S(2)}) copy-start(s32[896]{0:T(1024)S(1)} %get-tuple-element.109) | copy-start | bytes 10756
  15.6 9.2 all-to-all-start
  25.4 8.7 all-to-all-start.1
  34.8 7.4 collective-permute-start.3
  36.7 5.8 collective-permute-start.2
  62.3 7.1 collective-permute-start.4
  65.2 5.9 collective-permute-start.5
  74.2 8.7 all-to-all-start.2
  162.4 5.7 collective-permute-start.7
  164.4 5.8 collective-permute-start.6
  188.4 6.0 collective-permute-start.8
  190.3 5.6 collective-permute-start.9
  199.0 8.7 all-to-all-start.4
  279.3 5.6 collective-permute-start.11
  281.3 5.8 collective-permute-start.10
  305.3 6.0 collective-permute-start.12
  307.2 5.6 collective-permute-start.13
  315.8 8.7 all-to-all-start.6
  387.0 119.7 %copy-start.15 = (f32[15,128]{1,0:T(8,128)}, f32[15,128]{1,0:T(8,128)S(1)}, u32[]{:S(2)}) copy-start(f32[15,128]{1,0:T(8,128)S(1)} %get-tuple-element.87) | copy-start | bytes 23044
  398.4 5.6 collective-permute-start.15
  400.4 5.8 collective-permute-start.14
  424.4 6.0 collective-permute-start.16
  426.3 5.6 collective-permute-start.17
  436.3 9.4 all-to-all-start.8
  518.0 5.6 collective-permute-start.19
  520.1 5.8 collective-permute-start.18
  544.1 6.0 collective-permute-start.20
  546.0 5.6 collective-permute-start.21
  555.9 9.8 all-to-all-start.10
  635.0 127.9 %copy-start.12 = (f32[15,128]{1,0:T(8,128)}, f32[15,128]{1,0:T(8,128)S(1)}, u32[]{:S(2)}) copy-start(f32[15,128]{1,0:T(8,128)S(1)} %get-tuple-element.84) | copy-start | bytes 23044
  646.3 5.6 collective-permute-start.23
  648.4 5.8 collective-permute-start.22
  672.3 6.0 collective-permute-start.24
  674.3 5.6 collective-permute-start.25
  684.2 9.4 all-to-all-start.12
  696.3 92.0 %copy-start.10 = (f32[15,128]{1,0:T(8,128)}, f32[15,128]{1,0:T(8,128)S(1)}, u32[]{:S(2)}) copy-start(f32[15,128]{1,0:T(8,128)S(1)} %get-tuple-element.82) | copy-start | bytes 23044
  774.2 5.6 collective-permute-start.27
  776.2 5.8 collective-permute-start.26
  800.4 6.0 collective-permute-start.28
  802.3 5.6 collective-permute-start.29
  812.3 9.4 all-to-all-start.14
  916.6 5.6 collective-permute-start.31
  918.7 5.8 collective-permute-start.30
  942.6 6.0 collective-permute-start.32
  944.6 5.6 collective-permute-start.33
  954.5 9.4 all-to-all-start.16
  (23 other events, 476.1 us)
